TPU v7x, 32 devices: a whole 2x2x4 slice. The times are simulated.
32 devices in a mesh: grp: 2 (over y), shard: 16 (over z, x, core).
Axes of the slice: x: 2, y: 2, z: 4, core: 2. Of those that a mesh axis runs over, the one named last changes fastest.
Arguments:
- projections: bfloat16 [3, 4096, 512], P(None, ('grp', 'shard')), may hold values from -6 to 6
- short_taps: float32 [3, 7, 512], replicated, may hold values from -2 to 2
- long_filter: float32 [4096, 512], P(('grp', 'shard')), may hold values from -0.09375 to 0.09375
- skip_gain: float32 [512], replicated, may hold values from 0.5 to 1.5
Outputs:
- output: bfloat16 [4096, 512], P(('grp', 'shard'))
All inputs are finite; a program needn't handle non-finite values.
Results may differ from a plain program's by a relative error of at most 0.001.
Values may be sent and summed in bfloat16 or wider, within the bound.
A program may use at most 64 MiB of HBM per device.

v0:
```python
import math

import jax
import jax.numpy as jnp
from jax import lax
from jax.sharding import PartitionSpec as P

precise = lax.Precision.HIGHEST


def from_behind(block, axis, distance):
    devices = range(lax.axis_size(axis))
    route = [(i - distance, i) for i in devices if i - distance in devices]
    return lax.ppermute(block, axis, route)


def angles_of(first, second, modulus):
    return (first * second % modulus).astype(jnp.float32) * (2.0 * math.pi / modulus)


def per_device(projections, short_taps, long_filter, skip_gain):
    positions = projections.shape[1]
    channels = projections.shape[2]
    taps_count = short_taps.shape[1]
    groups = lax.axis_size("grp")
    shards = lax.axis_size("shard")
    devices = groups * shards
    span_len = 2 * devices
    length = span_len * positions
    slice_len = positions * channels // devices
    device_id = lax.axis_index("grp") * shards + lax.axis_index("shard")
    rim_rows = from_behind(projections[:, positions - (taps_count - 1) :, :], ("grp", "shard"), 1)
    extended = jnp.concatenate([rim_rows, projections], axis=1)
    shortened = short_taps[:, 0, None, :] * extended[
        :, taps_count - 1 : taps_count - 1 + positions, :
    ].astype(jnp.float32)
    for tap_index in range(1, taps_count):
        shortened = shortened + short_taps[:, tap_index, None, :] * extended[
            :, taps_count - 1 - tap_index : taps_count - 1 - tap_index + positions, :
        ].astype(jnp.float32)
    query = shortened[0]
    mixed = shortened[1] * shortened[2]
    mixed_rows = mixed.reshape(groups, shards, slice_len)
    filt_rows = long_filter.reshape(groups, shards, slice_len)
    got_mixed, got_filt = (
        lax.all_to_all(
            lax.all_to_all(mixed_rows, "grp", split_axis=0, concat_axis=0, tiled=True),
            "shard",
            split_axis=1,
            concat_axis=1,
            tiled=True,
        ),
        lax.all_to_all(
            lax.all_to_all(filt_rows, "grp", split_axis=0, concat_axis=0, tiled=True),
            "shard",
            split_axis=1,
            concat_axis=1,
            tiled=True,
        ),
    )
    dev_ids = jnp.arange(devices, dtype=jnp.int32)
    freq_ids = jnp.arange(span_len, dtype=jnp.int32)
    outer = angles_of(freq_ids[:, None], dev_ids[None, :], span_len)
    outer_cos, outer_sin = (jnp.cos(outer), jnp.sin(outer))
    flat_ids = device_id * slice_len + jnp.arange(slice_len, dtype=jnp.int32)
    row_of = flat_ids // channels
    twist = angles_of(freq_ids[:, None], row_of[None, :], length)
    twist_cos, twist_sin = (jnp.cos(twist), jnp.sin(twist))

    def forward_outer(values):
        flat_values = values.reshape(devices, slice_len)
        real = jnp.dot(outer_cos, flat_values, precision=precise)
        imag = -jnp.dot(outer_sin, flat_values, precision=precise)
        turned_re = real * twist_cos + imag * twist_sin
        turned_im = imag * twist_cos - real * twist_sin
        return (
            turned_re.reshape(2, groups, shards, slice_len),
            turned_im.reshape(2, groups, shards, slice_len),
        )

    mixed_re, mixed_im = forward_outer(got_mixed)
    filt_re, filt_im = forward_outer(got_filt)
    mixed_re, mixed_im, filt_re, filt_im = (
        lax.all_to_all(
            lax.all_to_all(mixed_re, "grp", split_axis=1, concat_axis=1, tiled=True),
            "shard",
            split_axis=2,
            concat_axis=2,
            tiled=True,
        ),
        lax.all_to_all(
            lax.all_to_all(mixed_im, "grp", split_axis=1, concat_axis=1, tiled=True),
            "shard",
            split_axis=2,
            concat_axis=2,
            tiled=True,
        ),
        lax.all_to_all(
            lax.all_to_all(filt_re, "grp", split_axis=1, concat_axis=1, tiled=True),
            "shard",
            split_axis=2,
            concat_axis=2,
            tiled=True,
        ),
        lax.all_to_all(
            lax.all_to_all(filt_im, "grp", split_axis=1, concat_axis=1, tiled=True),
            "shard",
            split_axis=2,
            concat_axis=2,
            tiled=True,
        ),
    )
    row_ids = jnp.arange(positions, dtype=jnp.int32)
    inner = angles_of(row_ids[:, None], row_ids[None, :], positions)
    inner_cos, inner_sin = (jnp.cos(inner), jnp.sin(inner))

    def forward_inner(real, imag):
        real = real.reshape(2, positions, channels)
        imag = imag.reshape(2, positions, channels)
        out_re = jnp.einsum("kp,rpc->rkc", inner_cos, real, precision=precise) + jnp.einsum(
            "kp,rpc->rkc", inner_sin, imag, precision=precise
        )
        out_im = jnp.einsum("kp,rpc->rkc", inner_cos, imag, precision=precise) - jnp.einsum(
            "kp,rpc->rkc", inner_sin, real, precision=precise
        )
        return (out_re, out_im)

    spec_mixed_re, spec_mixed_im = forward_inner(mixed_re, mixed_im)
    spec_filt_re, spec_filt_im = forward_inner(filt_re, filt_im)
    prod_re = spec_mixed_re * spec_filt_re - spec_mixed_im * spec_filt_im
    prod_im = spec_mixed_re * spec_filt_im + spec_mixed_im * spec_filt_re
    back_re = jnp.einsum("kp,rkc->rpc", inner_cos, prod_re, precision=precise) - jnp.einsum(
        "kp,rkc->rpc", inner_sin, prod_im, precision=precise
    )
    back_im = jnp.einsum("kp,rkc->rpc", inner_cos, prod_im, precision=precise) + jnp.einsum(
        "kp,rkc->rpc", inner_sin, prod_re, precision=precise
    )
    own_freqs = jnp.arange(2, dtype=jnp.int32) * devices + device_id
    back_twist = angles_of(own_freqs[:, None], row_ids[None, :], length)
    back_cos, back_sin = (jnp.cos(back_twist)[:, :, None], jnp.sin(back_twist)[:, :, None])
    rot_re = (back_re * back_cos - back_im * back_sin).reshape(2, groups, shards, slice_len)
    rot_im = (back_re * back_sin + back_im * back_cos).reshape(2, groups, shards, slice_len)
    rot_re, rot_im = (
        lax.all_to_all(
            lax.all_to_all(rot_re, "grp", split_axis=1, concat_axis=1, tiled=True),
            "shard",
            split_axis=2,
            concat_axis=2,
            tiled=True,
        ),
        lax.all_to_all(
            lax.all_to_all(rot_im, "grp", split_axis=1, concat_axis=1, tiled=True),
            "shard",
            split_axis=2,
            concat_axis=2,
            tiled=True,
        ),
    )
    rot_re = rot_re.reshape(span_len, slice_len)
    rot_im = rot_im.reshape(span_len, slice_len)
    values = (
        jnp.einsum("kd,kf->df", outer_cos, rot_re, precision=precise)
        - jnp.einsum("kd,kf->df", outer_sin, rot_im, precision=precise)
    ) / length
    values = values.reshape(groups, shards, slice_len)
    conv_rows = lax.all_to_all(
        lax.all_to_all(values, "grp", split_axis=0, concat_axis=0, tiled=True),
        "shard",
        split_axis=1,
        concat_axis=1,
        tiled=True,
    )
    conv = conv_rows.reshape(positions, channels)
    return (query * (conv + skip_gain * mixed)).astype(jnp.bfloat16)


def solution(mesh):
    placed = (P(None, ("grp", "shard"), None), P(), P(("grp", "shard"), None), P())
    return jax.shard_map(
        per_device, mesh=mesh, in_specs=placed, out_specs=P(("grp", "shard"), None), check_vma=False
    )
```

profile of v0, /device:TPU:0, one launch (start us, length us, event | category | flops | bytes accessed | tf_op | source)
XLA Modules:
  0.0 271.9 jit_solution(3283996681328900480)
XLA Ops:
  0.7 2.4 collective-permute-start
  3.1 1.8 reshape.139
  4.9 3.9 %all-to-all-start.6 = ((f32[2,16,2048]{2,1,0:T(8,128)}), f32[2,16,2048]{2,1,0:T(8,128)S(1)}, u32[]{:S(2)}, u32[]{:S(2)}) async-start(f32[2,16,2048]{2,1,0:T(8,128)} %reshape.139), calls=%async_computation.6 | async-start | bytes 524288 | tf_op jit(solution)/shard_map/all_to_all | solution.py:54
  10.5 3.9 %all-to-all-done.6 = f32[2,16,2048]{2,1,0:T(8,128)S(1)} async-done(((f32[2,16,2048]{2,1,0:T(8,128)}), f32[2,16,2048]{2,1,0:T(8,128)S(1)}, u32[]{:S(2)}, u32[]{:S(2)}) %all-to-all-start.6) | async-done | bytes 262176 | tf_op jit(solution)/shard_map/all_to_all | solution.py:54
  14.4 3.4 %all-to-all-start = ((f32[2,16,2048]{2,1,0:T(8,128)}), f32[2,16,2048]{2,1,0:T(8,128)S(1)}, u32[]{:S(2)}, u32[]{:S(2)}) async-start(f32[2,16,2048]{2,1,0:T(8,128)} %mul.421), calls=%async_computation | async-start | bytes 524288 | tf_op jit(solution)/shard_map/all_to_all | solution.py:47
  18.8 5.6 %all-to-all-done = f32[2,16,2048]{2,1,0:T(8,128)S(1)} async-done(((f32[2,16,2048]{2,1,0:T(8,128)}), f32[2,16,2048]{2,1,0:T(8,128)S(1)}, u32[]{:S(2)}, u32[]{:S(2)}) %all-to-all-start) | async-done | bytes 262176 | tf_op jit(solution)/shard_map/all_to_all | solution.py:47
  24.4 6.4 %all-to-all-start.7 = ((f32[2,16,2048]{2,0,1:T(2,128)}), f32[2,16,2048]{2,0,1:T(2,128)S(1)}, u32[]{:S(2)}, u32[]{:S(2)}) async-start(f32[2,16,2048]{2,0,1:T(2,128)} %copy.86), calls=%async_computation.7 | async-start | bytes 524288 | tf_op jit(solution)/shard_map/all_to_all | solution.py:53
  31.8 9.1 %all-to-all-done.7 = f32[2,16,2048]{2,0,1:T(2,128)S(1)} async-done(((f32[2,16,2048]{2,0,1:T(2,128)}), f32[2,16,2048]{2,0,1:T(2,128)S(1)}, u32[]{:S(2)}, u32[]{:S(2)}) %all-to-all-start.7) | async-done | bytes 262176 | tf_op jit(solution)/shard_map/all_to_all | solution.py:53
  40.9 3.5 %all-to-all-start.1 = ((f32[2,16,2048]{2,0,1:T(2,128)}), f32[2,16,2048]{2,0,1:T(2,128)S(1)}, u32[]{:S(2)}, u32[]{:S(2)}) async-start(f32[2,16,2048]{2,0,1:T(2,128)} %copy.76), calls=%async_computation.1 | async-start | bytes 524288 | tf_op jit(solution)/shard_map/all_to_all | solution.py:46
  45.3 9.1 %all-to-all-done.1 = f32[2,16,2048]{2,0,1:T(2,128)S(1)} async-done(((f32[2,16,2048]{2,0,1:T(2,128)}), f32[2,16,2048]{2,0,1:T(2,128)S(1)}, u32[]{:S(2)}, u32[]{:S(2)}) %all-to-all-start.1) | async-done | bytes 262176 | tf_op jit(solution)/shard_map/all_to_all | solution.py:46
  55.9 2.8 %multiply_subtract_fusion.1 = (f32[64,2048]{1,0:T(8,128)S(1)}, f32[64,2048]{1,0:T(8,128)S(1)}, f32[64,2048]{1,0:T(8,128)S(1)}, f32[64,2048]{1,0:T(8,128)S(1)}) fusion(f32[64,2048]{1,0:T(8,128)S(1)} %convolution_negate_fusion, s32[2048]{0:T(1024)S(1)} %add_select_fusion.3, f32[64,2048]{1,0:T(8,128)S(1)} %fusion.71, ...), kind=kOutput, calls=%fused_computation.32 | convolution fusion | flops 53768192 | bytes 3940352 | tf_op jit(solution)/shard_map/dot_general | solution.py:72
  59.6 3.5 %all-to-all-start.8 = ((f32[2,2,16,2048]{3,2,0,1:T(8,128)}), f32[2,2,16,2048]{3,2,0,1:T(8,128)S(1)}, u32[]{:S(2)}, u32[]{:S(2)}) async-start(f32[2,2,16,2048]{3,2,0,1:T(8,128)} %copy.88), calls=%async_computation.8 | async-start | bytes 1048576 | tf_op jit(solution)/shard_map/all_to_all | solution.py:99
  63.9 7.4 %all-to-all-done.8 = f32[2,2,16,2048]{3,2,0,1:T(8,128)S(1)} async-done(((f32[2,2,16,2048]{3,2,0,1:T(8,128)}), f32[2,2,16,2048]{3,2,0,1:T(8,128)S(1)}, u32[]{:S(2)}, u32[]{:S(2)}) %all-to-all-start.8) | async-done | bytes 524320 | tf_op jit(solution)/shard_map/all_to_all | solution.py:99
  71.4 3.5 %all-to-all-start.10 = ((f32[2,2,16,2048]{3,2,0,1:T(8,128)}), f32[2,2,16,2048]{3,2,0,1:T(8,128)S(1)}, u32[]{:S(2)}, u32[]{:S(2)}) async-start(f32[2,2,16,2048]{3,2,0,1:T(8,128)} %copy.92), calls=%async_computation.10 | async-start | bytes 1048576 | tf_op jit(solution)/shard_map/all_to_all | solution.py:106
  75.7 6.6 %all-to-all-done.10 = f32[2,2,16,2048]{3,2,0,1:T(8,128)S(1)} async-done(((f32[2,2,16,2048]{3,2,0,1:T(8,128)}), f32[2,2,16,2048]{3,2,0,1:T(8,128)S(1)}, u32[]{:S(2)}, u32[]{:S(2)}) %all-to-all-start.10) | async-done | bytes 524320 | tf_op jit(solution)/shard_map/all_to_all | solution.py:106
  82.3 3.5 %all-to-all-start.4 = ((f32[2,2,16,2048]{3,2,0,1:T(8,128)}), f32[2,2,16,2048]{3,2,0,1:T(8,128)S(1)}, u32[]{:S(2)}, u32[]{:S(2)}) async-start(f32[2,2,16,2048]{3,2,0,1:T(8,128)} %copy.82), calls=%async_computation.4 | async-start | bytes 1048576 | tf_op jit(solution)/shard_map/all_to_all | solution.py:92
  86.6 5.7 %all-to-all-done.4 = f32[2,2,16,2048]{3,2,0,1:T(8,128)S(1)} async-done(((f32[2,2,16,2048]{3,2,0,1:T(8,128)}), f32[2,2,16,2048]{3,2,0,1:T(8,128)S(1)}, u32[]{:S(2)}, u32[]{:S(2)}) %all-to-all-start.4) | async-done | bytes 524320 | tf_op jit(solution)/shard_map/all_to_all | solution.py:92
  92.4 3.5 %all-to-all-start.2 = ((f32[2,2,16,2048]{3,2,0,1:T(8,128)}), f32[2,2,16,2048]{3,2,0,1:T(8,128)S(1)}, u32[]{:S(2)}, u32[]{:S(2)}) async-start(f32[2,2,16,2048]{3,2,0,1:T(8,128)} %copy.78), calls=%async_computation.2 | async-start | bytes 1048576 | tf_op jit(solution)/shard_map/all_to_all | solution.py:85
  95.9 1.2 copy.89
  97.1 5.3 %all-to-all-done.2 = f32[2,2,16,2048]{3,2,0,1:T(8,128)S(1)} async-done(((f32[2,2,16,2048]{3,2,0,1:T(8,128)}), f32[2,2,16,2048]{3,2,0,1:T(8,128)S(1)}, u32[]{:S(2)}, u32[]{:S(2)}) %all-to-all-start.2) | async-done | bytes 524320 | tf_op jit(solution)/shard_map/all_to_all | solution.py:85
  102.4 4.3 %all-to-all-start.9 = ((f32[2,2,16,2048]{3,1,0,2:T(2,128)}), f32[2,2,16,2048]{3,1,0,2:T(2,128)S(1)}, u32[]{:S(2)}, u32[]{:S(2)}) async-start(f32[2,2,16,2048]{3,1,0,2:T(2,128)} %copy.89), calls=%async_computation.9 | async-start | bytes 1048576 | tf_op jit(solution)/shard_map/all_to_all | solution.py:98
  106.7 1.2 copy.93
  107.9 13.1 %all-to-all-done.9 = f32[2,2,16,2048]{3,1,0,2:T(2,128)S(1)} async-done(((f32[2,2,16,2048]{3,1,0,2:T(2,128)}), f32[2,2,16,2048]{3,1,0,2:T(2,128)S(1)}, u32[]{:S(2)}, u32[]{:S(2)}) %all-to-all-start.9) | async-done | bytes 524320 | tf_op jit(solution)/shard_map/all_to_all | solution.py:98
  121.0 4.2 %all-to-all-start.11 = ((f32[2,2,16,2048]{3,1,0,2:T(2,128)}), f32[2,2,16,2048]{3,1,0,2:T(2,128)S(1)}, u32[]{:S(2)}, u32[]{:S(2)}) async-start(f32[2,2,16,2048]{3,1,0,2:T(2,128)} %copy.93), calls=%async_computation.11 | async-start | bytes 1048576 | tf_op jit(solution)/shard_map/all_to_all | solution.py:105
  125.2 1.2 copy.83
  126.4 13.1 %all-to-all-done.11 = f32[2,2,16,2048]{3,1,0,2:T(2,128)S(1)} async-done(((f32[2,2,16,2048]{3,1,0,2:T(2,128)}), f32[2,2,16,2048]{3,1,0,2:T(2,128)S(1)}, u32[]{:S(2)}, u32[]{:S(2)}) %all-to-all-start.11) | async-done | bytes 524320 | tf_op jit(solution)/shard_map/all_to_all | solution.py:105
  139.4 4.4 %all-to-all-start.5 = ((f32[2,2,16,2048]{3,1,0,2:T(2,128)}), f32[2,2,16,2048]{3,1,0,2:T(2,128)}, u32[]{:S(2)}, u32[]{:S(2)}) async-start(f32[2,2,16,2048]{3,1,0,2:T(2,128)} %copy.83), calls=%async_computation.5 | async-start | bytes 1048576 | tf_op jit(solution)/shard_map/all_to_all | solution.py:91
  144.0 1.2 copy.79
  147.3 10.7 %all-to-all-done.5 = f32[2,2,16,2048]{3,1,0,2:T(2,128)} async-done(((f32[2,2,16,2048]{3,1,0,2:T(2,128)}), f32[2,2,16,2048]{3,1,0,2:T(2,128)}, u32[]{:S(2)}, u32[]{:S(2)}) %all-to-all-start.5) | async-done | bytes 524320 | tf_op jit(solution)/shard_map/all_to_all | solution.py:91
  158.0 4.2 %all-to-all-start.3 = ((f32[2,2,16,2048]{3,1,0,2:T(2,128)}), f32[2,2,16,2048]{3,1,0,2:T(2,128)}, u32[]{:S(2)}, u32[]{:S(2)}) async-start(f32[2,2,16,2048]{3,1,0,2:T(2,128)} %copy.79), calls=%async_computation.3 | async-start | bytes 1048576 | tf_op jit(solution)/shard_map/all_to_all | solution.py:84
  162.2 1.3 copy.84
  164.9 1.9 fusion.36
  167.9 1.1 convolution_add_fusion.1
  169.0 7.5 %all-to-all-done.3 = f32[2,2,16,2048]{3,1,0,2:T(2,128)} async-done(((f32[2,2,16,2048]{3,1,0,2:T(2,128)}), f32[2,2,16,2048]{3,1,0,2:T(2,128)}, u32[]{:S(2)}, u32[]{:S(2)}) %all-to-all-start.3) | async-done | bytes 524320 | tf_op jit(solution)/shard_map/all_to_all | solution.py:84
  176.5 1.3 copy.80
  180.3 1.1 multiply_subtract_fusion
  186.3 3.5 %all-to-all-start.12 = ((f32[2,2,16,2048]{3,2,0,1:T(8,128)}), f32[2,2,16,2048]{3,2,0,1:T(8,128)S(1)}, u32[]{:S(2)}, u32[]{:S(2)}) async-start(f32[2,2,16,2048]{3,2,0,1:T(8,128)} %copy.101), calls=%async_computation.12 | async-start | bytes 1048576 | tf_op jit(solution)/shard_map/all_to_all | solution.py:145
  191.1 7.2 %all-to-all-done.12 = f32[2,2,16,2048]{3,2,0,1:T(8,128)S(1)} async-done(((f32[2,2,16,2048]{3,2,0,1:T(8,128)}), f32[2,2,16,2048]{3,2,0,1:T(8,128)S(1)}, u32[]{:S(2)}, u32[]{:S(2)}) %all-to-all-start.12) | async-done | bytes 524320 | tf_op jit(solution)/shard_map/all_to_all | solution.py:145
  198.3 3.5 %all-to-all-start.14 = ((f32[2,2,16,2048]{3,2,0,1:T(8,128)}), f32[2,2,16,2048]{3,2,0,1:T(8,128)S(1)}, u32[]{:S(2)}, u32[]{:S(2)}) async-start(f32[2,2,16,2048]{3,2,0,1:T(8,128)} %copy.105), calls=%async_computation.14 | async-start | bytes 1048576 | tf_op jit(solution)/shard_map/all_to_all | solution.py:152
  201.8 1.2 copy.102
  203.0 6.5 %all-to-all-done.14 = f32[2,2,16,2048]{3,2,0,1:T(8,128)S(1)} async-done(((f32[2,2,16,2048]{3,2,0,1:T(8,128)}), f32[2,2,16,2048]{3,2,0,1:T(8,128)S(1)}, u32[]{:S(2)}, u32[]{:S(2)}) %all-to-all-start.14) | async-done | bytes 524320 | tf_op jit(solution)/shard_map/all_to_all | solution.py:152
  209.5 4.7 %all-to-all-start.13 = ((f32[2,2,16,2048]{3,1,0,2:T(2,128)}), f32[2,2,16,2048]{3,1,0,2:T(2,128)S(1)}, u32[]{:S(2)}, u32[]{:S(2)}) async-start(f32[2,2,16,2048]{3,1,0,2:T(2,128)} %copy.102), calls=%async_computation.13 | async-start | bytes 1048576 | tf_op jit(solution)/shard_map/all_to_all | solution.py:144
  214.1 1.2 copy.106
  215.4 13.1 %all-to-all-done.13 = f32[2,2,16,2048]{3,1,0,2:T(2,128)S(1)} async-done(((f32[2,2,16,2048]{3,1,0,2:T(2,128)}), f32[2,2,16,2048]{3,1,0,2:T(2,128)S(1)}, u32[]{:S(2)}, u32[]{:S(2)}) %all-to-all-start.13) | async-done | bytes 524320 | tf_op jit(solution)/shard_map/all_to_all | solution.py:144
  228.4 4.2 %all-to-all-start.15 = ((f32[2,2,16,2048]{3,1,0,2:T(2,128)}), f32[2,2,16,2048]{3,1,0,2:T(2,128)S(1)}, u32[]{:S(2)}, u32[]{:S(2)}) async-start(f32[2,2,16,2048]{3,1,0,2:T(2,128)} %copy.106), calls=%async_computation.15 | async-start | bytes 1048576 | tf_op jit(solution)/shard_map/all_to_all | solution.py:151
  233.5 13.4 %all-to-all-done.15 = f32[2,2,16,2048]{3,1,0,2:T(2,128)S(1)} async-done(((f32[2,2,16,2048]{3,1,0,2:T(2,128)}), f32[2,2,16,2048]{3,1,0,2:T(2,128)S(1)}, u32[]{:S(2)}, u32[]{:S(2)}) %all-to-all-start.15) | async-done | bytes 524320 | tf_op jit(solution)/shard_map/all_to_all | solution.py:151
  247.7 8.1 %all_to_all.90 = f32[2,16,2048]{2,1,0:T(8,128)S(1)} all-to-all(f32[2,16,2048]{2,1,0:T(8,128)S(1)} %bitcast.114), channel_id=1, replica_groups=mesh['grp'=2,'shard'=16] {'grp'}, dimensions={0} | all-to-all | bytes 524288 | tf_op jit(solution)/shard_map/all_to_all | solution.py:167
  256.1 14.2 %all_to_all.91 = f32[2,16,2048]{2,0,1:T(2,128)S(1)} all-to-all(f32[2,16,2048]{2,0,1:T(2,128)S(1)} %copy.108), channel_id=1, replica_groups=mesh['grp'=2,'shard'=16] {'shard'}, dimensions={1} | all-to-all | bytes 524288 | tf_op jit(solution)/shard_map/all_to_all | solution.py:166
  (61 shorter events, 26.4 us)
Async XLA Ops:
  0.7 8.2 %collective-permute-start = (bf16[3,6,512]{2,1,0:T(8,128)(2,1)S(1)}, bf16[3,6,512]{2,1,0:T(8,128)(2,1)S(1)}, u32[]{:S(2)}, u32[]{:S(2)}) collective-permute-start(bf16[3,6,512]{2,1,0:T(8,128)(2,1)S(1)} %slice.53), channel_id=1, source_target_pairs={{0,1},{1,2},{2,3},{3,4},{4,5},{5,6},{6,7},{7,8},{8,9},{9,10},{10,1... | collective-permute-start | bytes 55304 | tf_op jit(solution)/shard_map/ppermute | solution.py:14
  4.9 3.9 %copy-start.2 = (f32[3,7,512]{2,1,0:T(8,128)S(1)}, f32[3,7,512]{2,1,0:T(8,128)}, u32[]{:S(2)}) copy-start(f32[3,7,512]{2,1,0:T(8,128)} %param.5) | copy-start | bytes 129028
  4.9 4.0 %copy-start.1 = (bf16[3,128,512]{2,1,0:T(8,128)(2,1)S(1)}, bf16[3,128,512]{2,1,0:T(8,128)(2,1)}, u32[]{:S(2)}) copy-start(bf16[3,128,512]{2,1,0:T(8,128)(2,1)} %param.4) | copy-start | bytes 1179652
  4.9 9.5 %all-to-all-start.6 = ((f32[2,16,2048]{2,1,0:T(8,128)}), f32[2,16,2048]{2,1,0:T(8,128)S(1)}, u32[]{:S(2)}, u32[]{:S(2)}) async-start(f32[2,16,2048]{2,1,0:T(8,128)} %reshape.139), calls=%async_computation.6 | async-start | bytes 524288 | tf_op jit(solution)/shard_map/all_to_all | solution.py:54
  14.4 10.0 %all-to-all-start = ((f32[2,16,2048]{2,1,0:T(8,128)}), f32[2,16,2048]{2,1,0:T(8,128)S(1)}, u32[]{:S(2)}, u32[]{:S(2)}) async-start(f32[2,16,2048]{2,1,0:T(8,128)} %mul.421), calls=%async_computation | async-start | bytes 524288 | tf_op jit(solution)/shard_map/all_to_all | solution.py:47
  24.4 16.4 %all-to-all-start.7 = ((f32[2,16,2048]{2,0,1:T(2,128)}), f32[2,16,2048]{2,0,1:T(2,128)S(1)}, u32[]{:S(2)}, u32[]{:S(2)}) async-start(f32[2,16,2048]{2,0,1:T(2,128)} %copy.86), calls=%async_computation.7 | async-start | bytes 524288 | tf_op jit(solution)/shard_map/all_to_all | solution.py:53
  40.9 13.5 %all-to-all-start.1 = ((f32[2,16,2048]{2,0,1:T(2,128)}), f32[2,16,2048]{2,0,1:T(2,128)S(1)}, u32[]{:S(2)}, u32[]{:S(2)}) async-start(f32[2,16,2048]{2,0,1:T(2,128)} %copy.76), calls=%async_computation.1 | async-start | bytes 524288 | tf_op jit(solution)/shard_map/all_to_all | solution.py:46
  59.6 11.8 %all-to-all-start.8 = ((f32[2,2,16,2048]{3,2,0,1:T(8,128)}), f32[2,2,16,2048]{3,2,0,1:T(8,128)S(1)}, u32[]{:S(2)}, u32[]{:S(2)}) async-start(f32[2,2,16,2048]{3,2,0,1:T(8,128)} %copy.88), calls=%async_computation.8 | async-start | bytes 1048576 | tf_op jit(solution)/shard_map/all_to_all | solution.py:99
  71.4 10.9 %all-to-all-start.10 = ((f32[2,2,16,2048]{3,2,0,1:T(8,128)}), f32[2,2,16,2048]{3,2,0,1:T(8,128)S(1)}, u32[]{:S(2)}, u32[]{:S(2)}) async-start(f32[2,2,16,2048]{3,2,0,1:T(8,128)} %copy.92), calls=%async_computation.10 | async-start | bytes 1048576 | tf_op jit(solution)/shard_map/all_to_all | solution.py:106
  82.3 10.1 %all-to-all-start.4 = ((f32[2,2,16,2048]{3,2,0,1:T(8,128)}), f32[2,2,16,2048]{3,2,0,1:T(8,128)S(1)}, u32[]{:S(2)}, u32[]{:S(2)}) async-start(f32[2,2,16,2048]{3,2,0,1:T(8,128)} %copy.82), calls=%async_computation.4 | async-start | bytes 1048576 | tf_op jit(solution)/shard_map/all_to_all | solution.py:92
  92.4 10.1 %all-to-all-start.2 = ((f32[2,2,16,2048]{3,2,0,1:T(8,128)}), f32[2,2,16,2048]{3,2,0,1:T(8,128)S(1)}, u32[]{:S(2)}, u32[]{:S(2)}) async-start(f32[2,2,16,2048]{3,2,0,1:T(8,128)} %copy.78), calls=%async_computation.2 | async-start | bytes 1048576 | tf_op jit(solution)/shard_map/all_to_all | solution.py:85
  102.4 18.5 %all-to-all-start.9 = ((f32[2,2,16,2048]{3,1,0,2:T(2,128)}), f32[2,2,16,2048]{3,1,0,2:T(2,128)S(1)}, u32[]{:S(2)}, u32[]{:S(2)}) async-start(f32[2,2,16,2048]{3,1,0,2:T(2,128)} %copy.89), calls=%async_computation.9 | async-start | bytes 1048576 | tf_op jit(solution)/shard_map/all_to_all | solution.py:98
  121.0 18.4 %all-to-all-start.11 = ((f32[2,2,16,2048]{3,1,0,2:T(2,128)}), f32[2,2,16,2048]{3,1,0,2:T(2,128)S(1)}, u32[]{:S(2)}, u32[]{:S(2)}) async-start(f32[2,2,16,2048]{3,1,0,2:T(2,128)} %copy.93), calls=%async_computation.11 | async-start | bytes 1048576 | tf_op jit(solution)/shard_map/all_to_all | solution.py:105
  139.4 18.5 %all-to-all-start.5 = ((f32[2,2,16,2048]{3,1,0,2:T(2,128)}), f32[2,2,16,2048]{3,1,0,2:T(2,128)}, u32[]{:S(2)}, u32[]{:S(2)}) async-start(f32[2,2,16,2048]{3,1,0,2:T(2,128)} %copy.83), calls=%async_computation.5 | async-start | bytes 1048576 | tf_op jit(solution)/shard_map/all_to_all | solution.py:91
  158.0 18.5 %all-to-all-start.3 = ((f32[2,2,16,2048]{3,1,0,2:T(2,128)}), f32[2,2,16,2048]{3,1,0,2:T(2,128)}, u32[]{:S(2)}, u32[]{:S(2)}) async-start(f32[2,2,16,2048]{3,1,0,2:T(2,128)} %copy.79), calls=%async_computation.3 | async-start | bytes 1048576 | tf_op jit(solution)/shard_map/all_to_all | solution.py:84
  179.1 1.1 copy-start
  186.3 12.0 %all-to-all-start.12 = ((f32[2,2,16,2048]{3,2,0,1:T(8,128)}), f32[2,2,16,2048]{3,2,0,1:T(8,128)S(1)}, u32[]{:S(2)}, u32[]{:S(2)}) async-start(f32[2,2,16,2048]{3,2,0,1:T(8,128)} %copy.101), calls=%async_computation.12 | async-start | bytes 1048576 | tf_op jit(solution)/shard_map/all_to_all | solution.py:145
  198.3 11.2 %all-to-all-start.14 = ((f32[2,2,16,2048]{3,2,0,1:T(8,128)}), f32[2,2,16,2048]{3,2,0,1:T(8,128)S(1)}, u32[]{:S(2)}, u32[]{:S(2)}) async-start(f32[2,2,16,2048]{3,2,0,1:T(8,128)} %copy.105), calls=%async_computation.14 | async-start | bytes 1048576 | tf_op jit(solution)/shard_map/all_to_all | solution.py:152
  209.5 19.0 %all-to-all-start.13 = ((f32[2,2,16,2048]{3,1,0,2:T(2,128)}), f32[2,2,16,2048]{3,1,0,2:T(2,128)S(1)}, u32[]{:S(2)}, u32[]{:S(2)}) async-start(f32[2,2,16,2048]{3,1,0,2:T(2,128)} %copy.102), calls=%async_computation.13 | async-start | bytes 1048576 | tf_op jit(solution)/shard_map/all_to_all | solution.py:144
  228.4 18.4 %all-to-all-start.15 = ((f32[2,2,16,2048]{3,1,0,2:T(2,128)}), f32[2,2,16,2048]{3,1,0,2:T(2,128)S(1)}, u32[]{:S(2)}, u32[]{:S(2)}) async-start(f32[2,2,16,2048]{3,1,0,2:T(2,128)} %copy.106), calls=%async_computation.15 | async-start | bytes 1048576 | tf_op jit(solution)/shard_map/all_to_all | solution.py:151
  270.5 0.7 copy-start.3
where the time goes:
time: 274 us; the launch traced here: 272 us
  waiting for transfers between devices  137 us (50%)
  starting transfers between devices  66.6 us (24%)
  local copies, waits for them, and re-layouts  24.3 us (9%)
  blocking collectives  22.4 us (8%)
  matrix products  19.3 us (7%)
    all_to_all x1, blocking collectives, per_device(): lax.all_to_all(lax.all_to_all(values, 'grp', split_axis=0, concat_axis=0,...  14.2 us
    all_to_all x1, waiting for transfers between devices, per_device(): lax.all_to_all(lax.all_to_all(rot_im, 'grp', split_axis=1, concat_axis=1,...  13.4 us
    all_to_all x1, waiting for transfers between devices, per_device(): lax.all_to_all(lax.all_to_all(filt_re, 'grp', split_axis=1, concat_axis=1...  13.1 us
    all_to_all x1, waiting for transfers between devices, per_device(): lax.all_to_all(lax.all_to_all(filt_im, 'grp', split_axis=1, concat_axis=1...  13.1 us
    all_to_all x1, waiting for transfers between devices, per_device(): lax.all_to_all(lax.all_to_all(rot_re, 'grp', split_axis=1, concat_axis=1,...  13.1 us
    all_to_all x1, waiting for transfers between devices, per_device(): lax.all_to_all(lax.all_to_all(mixed_im, 'grp', split_axis=1, concat_axis=...  10.7 us
    all_to_all x1, waiting for transfers between devices, per_device(): lax.all_to_all(lax.all_to_all(filt_rows, 'grp', split_axis=0, concat_axis...  9.1 us
    all_to_all x1, waiting for transfers between devices, per_device(): lax.all_to_all(lax.all_to_all(mixed_rows, 'grp', split_axis=0, concat_axi...  9.09 us
  transfers between devices with their start and end apart: 17, of which 16 were waited for; matrix products, arithmetic and copies ran while one was open for 10% of the time, Pallas kernels for 0%

commit v1 on v0

--- a/solution.py
+++ b/solution.py
@@ -1,8 +1,12 @@
+import functools
 import math
 
 import jax
 import jax.numpy as jnp
+import numpy as np
 from jax import lax
+from jax.experimental import pallas as pl
+from jax.experimental.pallas import tpu as pltpu
 from jax.sharding import PartitionSpec as P
 
 precise = lax.Precision.HIGHEST
@@ -174,8 +178,321 @@
     return (query * (conv + skip_gain * mixed)).astype(jnp.bfloat16)
 
 
+MESH = pl.DeviceIdType.MESH
+LANES = 128
+SUB = 8
+HALO = 16
+
+
+def turned(value, numerator, denominator):
+    numerator %= denominator
+    real, imag = value
+    eighths, rest = divmod(8 * numerator, denominator)
+    if rest == 0:
+        half = math.sqrt(0.5)
+        if eighths == 0:
+            return (real, imag)
+        if eighths == 2:
+            return (-imag, real)
+        if eighths == 4:
+            return (-real, -imag)
+        if eighths == 6:
+            return (imag, -real)
+        if eighths == 1:
+            return ((real - imag) * half, (real + imag) * half)
+        if eighths == 3:
+            return ((real + imag) * -half, (real - imag) * half)
+        if eighths == 5:
+            return ((imag - real) * half, (real + imag) * -half)
+        return ((real + imag) * half, (imag - real) * half)
+    angle = 2.0 * math.pi * numerator / denominator
+    cos, sin = (math.cos(angle), math.sin(angle))
+    return (real * cos - imag * sin, real * sin + imag * cos)
+
+
+def fft(loads, sign):
+    count = len(loads)
+    if count == 1:
+        return [loads[0]()]
+    even, odd = (fft(loads[::2], sign), fft(loads[1::2], sign))
+    low, high = ([], [])
+    for k in range(count // 2):
+        moved = turned(odd[k], sign * k, count)
+        low.append((even[k][0] + moved[0], even[k][1] + moved[1]))
+        high.append((even[k][0] - moved[0], even[k][1] - moved[1]))
+    return low + high
+
+
+def dot3(values, table_hi, table_lo):
+    hi = values.astype(jnp.bfloat16)
+    lo = (values - hi.astype(jnp.float32)).astype(jnp.bfloat16)
+    dot = functools.partial(jnp.dot, preferred_element_type=jnp.float32)
+    return dot(hi, table_hi[...]) + (dot(lo, table_hi[...]) + dot(hi, table_lo[...]))
+
+
+def owner_kernel(
+    sizes,
+    proj_ref,
+    taps_ref,
+    filt_ref,
+    gain_ref,
+    fwd_hi,
+    fwd_lo,
+    inv_hi,
+    inv_lo,
+    twist_cos,
+    twist_sin,
+    out_ref,
+    rim,
+    ext,
+    query,
+    direct,
+    filt_out,
+    mix_out,
+    filt_in,
+    mix_in,
+    conv_out,
+    conv_in,
+    spec_a,
+    spec_h,
+    spec_g,
+    rim_sems,
+    send_sems,
+    recv_sems,
+):
+    groups, shards, positions, channels, taps = sizes
+    devices = groups * shards
+    owned = channels // devices
+    halves = owned // SUB
+    per_chunk = LANES // owned
+    chunks = channels // LANES
+    me = lax.axis_index("grp") * shards + lax.axis_index("shard")
+
+    def place(target):
+        return (target // shards, target % shards)
+
+    barrier = pltpu.get_barrier_semaphore()
+
+    @pl.loop(1, devices)
+    def _(step):
+        pl.semaphore_signal(
+            barrier, inc=1, device_id=place(lax.rem(me + step, devices)), device_id_type=MESH
+        )
+
+    def scatter_rows(chunk, turned_block, store):
+        for part in range(per_chunk):
+            for half in range(halves):
+                first = part * owned + half * SUB
+                store[half, chunk * per_chunk + part] = turned_block[first : first + SUB, :]
+
+    for chunk in range(chunks):
+        lanes = slice(chunk * LANES, (chunk + 1) * LANES)
+        scatter_rows(chunk, filt_ref[:, lanes].T, filt_out)
+        for which in range(3):
+            ext[which, chunk, HALO:, :] = proj_ref[which, :, lanes].astype(jnp.float32)
+
+    pl.semaphore_wait(barrier, devices - 1)
+
+    rim_copy = pltpu.make_async_remote_copy(
+        src_ref=proj_ref.at[:, positions - HALO :, :],
+        dst_ref=rim,
+        send_sem=rim_sems.at[0],
+        recv_sem=rim_sems.at[1],
+        device_id=place(lax.rem(me + 1, devices)),
+        device_id_type=MESH,
+    )
+    rim_copy.start()
+
+    def send_all(source, landing, kind, half):
+        @pl.loop(1, devices)
+        def _(step):
+            target = lax.rem(me + step, devices)
+            pltpu.make_async_remote_copy(
+                src_ref=source.at[half, target],
+                dst_ref=landing.at[half, me],
+                send_sem=send_sems.at[kind, half],
+                recv_sem=recv_sems.at[kind, half],
+                device_id=place(target),
+                device_id_type=MESH,
+            ).start()
+
+        landing[half, me] = source[half, me]
+
+    def wait_all(landing, sems, kind, half):
+        others = landing.at[half, pl.ds(0, devices - 1)]
+        pltpu.make_async_copy(others, others, sems.at[kind, half]).wait()
+
+    for half in range(halves):
+        send_all(filt_out, filt_in, 0, half)
+
+    rim_copy.wait()
+    keep = jnp.where(me > 0, 1.0, 0.0).astype(jnp.float32)
+    for chunk in range(chunks):
+        lanes = slice(chunk * LANES, (chunk + 1) * LANES)
+        for which in range(3):
+            ext[which, chunk, :HALO, :] = rim[which, :, lanes].astype(jnp.float32) * keep
+
+    def shortened(which, chunk):
+        lanes = slice(chunk * LANES, (chunk + 1) * LANES)
+        total = None
+        for tap in range(taps):
+            term = taps_ref[which, tap : tap + 1, lanes] * ext[
+                which, chunk, HALO - tap : HALO - tap + positions, :
+            ]
+            total = term if total is None else total + term
+        return total
+
+    for chunk in range(chunks):
+        mixed = shortened(1, chunk) * shortened(2, chunk)
+        direct[chunk] = mixed
+        scatter_rows(chunk, mixed.T, mix_out)
+    for half in range(halves):
+        send_all(mix_out, mix_in, 1, half)
+
+    for chunk in range(chunks):
+        lanes = slice(chunk * LANES, (chunk + 1) * LANES)
+        query[chunk] = shortened(0, chunk)
+        direct[chunk] = direct[chunk] * gain_ref[:, lanes]
+
+    def transform(landing, half):
+        def load(block):
+            def get():
+                value = landing[half, block]
+                angle = 2.0 * math.pi * block / (4 * devices)
+                return (value * math.cos(angle), value * math.sin(angle))
+
+            return get
+
+        for k, (real, imag) in enumerate(fft([load(b) for b in range(devices)], 1)):
+            cos, sin = (twist_cos[k : k + 1, :], twist_sin[k : k + 1, :])
+            rows = slice(k * SUB, (k + 1) * SUB)
+            spec_a[rows, :LANES] = real * cos - imag * sin
+            spec_a[rows, LANES:] = real * sin + imag * cos
+        return dot3(spec_a[...], fwd_hi, fwd_lo)
+
+    for half in range(halves):
+        wait_all(filt_in, recv_sems, 0, half)
+        spec_h[half] = transform(filt_in, half)
+
+    for half in range(halves):
+        wait_all(mix_in, recv_sems, 1, half)
+        mixed_spec = transform(mix_in, half)
+        mixed_re, mixed_im = (mixed_spec[:, :LANES], mixed_spec[:, LANES:])
+        filt_re, filt_im = (spec_h[half, :, :LANES], spec_h[half, :, LANES:])
+        spec_a[:, :LANES] = mixed_re * filt_re - mixed_im * filt_im
+        spec_a[:, LANES:] = mixed_re * filt_im + mixed_im * filt_re
+        spec_g[...] = dot3(spec_a[...], inv_hi, inv_lo)
+
+        def load(k):
+            def get():
+                rows = slice(k * SUB, (k + 1) * SUB)
+                real, imag = (spec_g[rows, :LANES], spec_g[rows, LANES:])
+                cos, sin = (twist_cos[k : k + 1, :], twist_sin[k : k + 1, :])
+                return (real * cos + imag * sin, imag * cos - real * sin)
+
+            return get
+
+        for block, (real, imag) in enumerate(fft([load(k) for k in range(devices)], -1)):
+            angle = 2.0 * math.pi * block / (4 * devices)
+            conv_out[half, block] = real * math.cos(angle) + imag * math.sin(angle)
+        send_all(conv_out, conv_in, 2, half)
+
+    for half in range(halves):
+        wait_all(conv_in, recv_sems, 2, half)
+    for chunk in range(chunks):
+        lanes = slice(chunk * LANES, (chunk + 1) * LANES)
+        pieces = [
+            conv_in[half, chunk * per_chunk + part]
+            for part in range(per_chunk)
+            for half in range(halves)
+        ]
+        conv = jnp.concatenate(pieces, axis=0).T
+        out_ref[:, lanes] = (query[chunk] * (conv + direct[chunk])).astype(out_ref.dtype)
+    for half in range(halves):
+        wait_all(filt_out, send_sems, 0, half)
+        wait_all(mix_out, send_sems, 1, half)
+        wait_all(conv_out, send_sems, 2, half)
+
+
+def split_table(table):
+    hi = table.astype(jnp.bfloat16)
+    lo = (table - hi.astype(np.float64)).astype(jnp.bfloat16)
+    return hi, lo
+
+
+def tables(devices, positions):
+    p = np.arange(positions, dtype=np.float64)
+    angle = 2.0 * np.pi * ((p[:, None] * p[None, :]) % positions) / positions
+    cos, sin = (np.cos(angle), np.sin(angle))
+    forward = np.block([[cos, sin], [-sin, cos]])
+    backward = np.block([[cos, -sin], [sin, cos]]) / (devices * positions)
+    k = np.arange(devices, dtype=np.float64)
+    twist = 2.0 * np.pi * (k[:, None] + 0.25) * p[None, :] / (devices * positions)
+    return (
+        *split_table(forward),
+        *split_table(backward),
+        np.cos(twist).astype(np.float32),
+        np.sin(twist).astype(np.float32),
+    )
+
+
+def owned_channels(consts, groups, shards, projections, short_taps, long_filter, skip_gain):
+    _, positions, channels = projections.shape
+    devices = groups * shards
+    owned = channels // devices
+    halves = owned // SUB
+    chunks = channels // LANES
+    sizes = (groups, shards, positions, channels, short_taps.shape[1])
+    f32, bf16 = (jnp.float32, jnp.bfloat16)
+    slabs = pltpu.VMEM((halves, devices, SUB, LANES), f32)
+    vmem = pl.BlockSpec(memory_space=pltpu.VMEM)
+    return pl.pallas_call(
+        functools.partial(owner_kernel, sizes),
+        out_shape=jax.ShapeDtypeStruct((positions, channels), bf16),
+        in_specs=[vmem] * (4 + len(consts)),
+        out_specs=vmem,
+        scratch_shapes=[
+            pltpu.VMEM((3, HALO, channels), bf16),
+            pltpu.VMEM((3, chunks, HALO + positions, LANES), f32),
+            pltpu.VMEM((chunks, positions, LANES), f32),
+            pltpu.VMEM((chunks, positions, LANES), f32),
+            slabs,
+            slabs,
+            slabs,
+            slabs,
+            slabs,
+            slabs,
+            pltpu.VMEM((devices * SUB, 2 * LANES), f32),
+            pltpu.VMEM((halves, devices * SUB, 2 * LANES), f32),
+            pltpu.VMEM((devices * SUB, 2 * LANES), f32),
+            pltpu.SemaphoreType.DMA((2,)),
+            pltpu.SemaphoreType.DMA((3, halves)),
+            pltpu.SemaphoreType.DMA((3, halves)),
+        ],
+        compiler_params=pltpu.CompilerParams(collective_id=0, has_side_effects=True),
+    )(projections, short_taps, long_filter, skip_gain.reshape(1, channels), *consts)
+
+
+def on_device(groups, shards, projections, short_taps, long_filter, skip_gain):
+    _, positions, channels = projections.shape
+    devices = groups * shards
+    fits = (
+        positions == LANES
+        and channels % LANES == 0
+        and channels % (SUB * devices) == 0
+        and LANES % (channels // devices) == 0
+        and devices & (devices - 1) == 0
+        and short_taps.shape[1] - 1 <= HALO
+    )
+    if not fits:
+        return per_device(projections, short_taps, long_filter, skip_gain)
+    consts = tables(devices, positions)
+    return owned_channels(consts, groups, shards, projections, short_taps, long_filter, skip_gain)
+
+
 def solution(mesh):
     placed = (P(None, ("grp", "shard"), None), P(), P(("grp", "shard"), None), P())
+    body = functools.partial(on_device, mesh.shape["grp"], mesh.shape["shard"])
     return jax.shard_map(
-        per_device, mesh=mesh, in_specs=placed, out_specs=P(("grp", "shard"), None), check_vma=False
-    )
+        body, mesh=mesh, in_specs=placed, out_specs=P(("grp", "shard"), None), check_vma=False
+    )

time: 274 us -> 31.7 us (0.12)
  waiting for transfers between devices: 137 us -> 0 us
  starting transfers between devices: 66.6 us -> 0 us
  Pallas kernels: 0 us -> 29.9 us
  local copies, waits for them, and re-layouts: 24.3 us -> 1.57 us
  blocking collectives: 22.4 us -> 0 us
  matrix products: 19.3 us -> 0 us
    all_to_all x16 -> x0, waiting for transfers between devices: 137 us -> none  [the longest x1 13.4 us: per_device(): lax.all_to_all(lax.all_to_all(rot_im, 'grp', split_axis=1, concat_axis=1,...]
    all_to_all x16 -> x0, starting transfers between devices: 64.2 us -> none  [the longest x1 6.42 us: per_device(): lax.all_to_all(lax.all_to_all(filt_rows, 'grp', split_axis=0, concat_axis...]
    pallas_call x0 -> x1, Pallas kernels: none -> 29.9 us  [owned_channels(): pl.pallas_call(functools.partial(owner_kernel, sizes), out_shape=jax.Shap...]
    all_to_all x2 -> x0, blocking collectives: 22.4 us -> none  [the longest x1 14.2 us: per_device(): lax.all_to_all(lax.all_to_all(values, 'grp', split_axis=0, concat_axis=0,...]
    dot_general x18 -> x0, matrix products: 19.3 us -> none  [the longest x2 3.51 us: forward_outer(): real = jnp.dot(outer_cos, flat_values, precision=precise)]
    all_to_all x18 -> x0, local copies, waits for them, and re-layouts: 13.7 us -> none  [the longest x1 1.35 us: per_device(): lax.all_to_all(lax.all_to_all(mixed_im, 'grp', split_axis=1, concat_axis=...]
    reshape x14 -> x0, local copies, waits for them, and re-layouts: 7.96 us -> none  [the longest x1 1.76 us: per_device(): filt_rows = long_filter.reshape(groups, shards, slice_len)]
  transfers between devices with their start and end apart: 17 -> 0, of which waited for: 16 -> 0; matrix products, arithmetic and copies ran while one was open for 10% -> 0% of each run, Pallas kernels for 0% -> 0%
where the time goes in v1:
time: 31.7 us; the launch traced here: 31.5 us
  Pallas kernels  29.9 us (94%)
  local copies, waits for them, and re-layouts  1.57 us (5%)
    pallas_call x1, Pallas kernels, owned_channels(): pl.pallas_call(functools.partial(owner_kernel, sizes), out_shape=jax.Shap...  29.9 us
    unnamed x1, local copies, waits for them, and re-layouts  1.57 us

profile of v1, /device:TPU:0, one launch (start us, length us, event | category | flops | bytes accessed | tf_op | source)
XLA Modules:
  0.0 31.5 jit_solution(14493079180634922956)
XLA Ops:
  0.0 29.9 %shard_map.100 = bf16[128,512]{1,0:T(8,128)(2,1)} custom-call(bf16[3,128,512]{2,1,0:T(8,128)(2,1)} %proj_ref.1, f32[3,7,512]{2,1,0:T(8,128)} %taps_ref.1, f32[128,512]{1,0:T(8,128)} %filt_ref.1, f32[1,512]{1,0:T(1,128)} %bitcast.1, bf16[256,256]{1,0:T(8,128)(2,1)} %constant.12.clone.fwd_hi, bf16[256,256]{1,0:T(8,128)(2,1)} %constant.13.clone.fwd_lo, ...), custom_call_target="tpu_custom_call" | custom-call | tf_op jit(solution)/shard_map/pallas_call | solution.py:449
  30.0 1.6 %copy.12 = bf16[128,512]{1,0:T(8,128)(2,1)} copy(bf16[128,512]{1,0:T(8,128)(2,1)} %shard_map.100) | data formatting | bytes 262144

commit v2 on v1

--- a/solution.py
+++ b/solution.py
@@ -182,6 +182,7 @@
 LANES = 128
 SUB = 8
 HALO = 16
+TOGETHER = 4
 
 
 def turned(value, numerator, denominator):
@@ -234,7 +235,7 @@
     sizes,
     proj_ref,
     taps_ref,
-    filt_ref,
+    held_ref,
     gain_ref,
     fwd_hi,
     fwd_lo,
@@ -248,13 +249,16 @@
     query,
     direct,
     filt_out,
-    mix_out,
+    pair_out,
     filt_in,
+    pair_in,
     mix_in,
+    tap_rows,
+    tap_columns,
     conv_out,
     conv_in,
     spec_a,
-    spec_h,
+    spec_held,
     spec_g,
     rim_sems,
     send_sems,
@@ -266,18 +270,24 @@
     halves = owned // SUB
     per_chunk = LANES // owned
     chunks = channels // LANES
-    me = lax.axis_index("grp") * shards + lax.axis_index("shard")
+    my_group, my_shard = (lax.axis_index("grp"), lax.axis_index("shard"))
+    me = my_group * shards + my_shard
+
+    def partners(act):
+        for apart in range(devices - 1, 0, -1):
+            group = jnp.bitwise_xor(my_group, apart // shards)
+            shard = jnp.bitwise_xor(my_shard, apart % shards)
+            act((group, shard), group * shards + shard)
 
     def place(target):
         return (target // shards, target % shards)
 
     barrier = pltpu.get_barrier_semaphore()
-
-    @pl.loop(1, devices)
-    def _(step):
-        pl.semaphore_signal(
-            barrier, inc=1, device_id=place(lax.rem(me + step, devices)), device_id_type=MESH
+    partners(
+        lambda there, target: pl.semaphore_signal(
+            barrier, inc=1, device_id=there, device_id_type=MESH
         )
+    )
 
     def scatter_rows(chunk, turned_block, store):
         for part in range(per_chunk):
@@ -287,9 +297,21 @@
 
     for chunk in range(chunks):
         lanes = slice(chunk * LANES, (chunk + 1) * LANES)
-        scatter_rows(chunk, filt_ref[:, lanes].T, filt_out)
+        scatter_rows(chunk, held_ref[:, lanes].T, filt_out)
         for which in range(3):
             ext[which, chunk, HALO:, :] = proj_ref[which, :, lanes].astype(jnp.float32)
+        tap_rows[...] = jnp.zeros_like(tap_rows)
+        for pair in range(2):
+            block = ext[pair + 1, chunk, HALO:, :].T.astype(jnp.bfloat16)
+            for part in range(per_chunk):
+                rows = slice(part * owned, (part + 1) * owned)
+                pair_out[pair, chunk * per_chunk + part] = block[rows, :]
+            tap_rows[pair * HALO : pair * HALO + taps, :] = taps_ref[pair + 1, :, lanes]
+        block = tap_rows[...].T
+        for part in range(per_chunk):
+            tap_columns[chunk * per_chunk + part] = block[part * owned : (part + 1) * owned, :]
+    for pair in range(2):
+        pair_in[pair, 0] = jnp.zeros((owned, LANES), jnp.bfloat16)
 
     pl.semaphore_wait(barrier, devices - 1)
 
@@ -301,29 +323,99 @@
         device_id=place(lax.rem(me + 1, devices)),
         device_id_type=MESH,
     )
-    rim_copy.start()
-
-    def send_all(source, landing, kind, half):
-        @pl.loop(1, devices)
-        def _(step):
-            target = lax.rem(me + step, devices)
+
+    def send_all(source, landing, kind, half, shift=0):
+        def send(there, target):
             pltpu.make_async_remote_copy(
                 src_ref=source.at[half, target],
-                dst_ref=landing.at[half, me],
+                dst_ref=landing.at[half, me + shift],
                 send_sem=send_sems.at[kind, half],
                 recv_sem=recv_sems.at[kind, half],
-                device_id=place(target),
+                device_id=there,
                 device_id_type=MESH,
             ).start()
 
-        landing[half, me] = source[half, me]
+        partners(send)
+        landing[half, me + shift] = source[half, me]
 
     def wait_all(landing, sems, kind, half):
         others = landing.at[half, pl.ds(0, devices - 1)]
         pltpu.make_async_copy(others, others, sems.at[kind, half]).wait()
 
+    for pair in range(2):
+        send_all(pair_out, pair_in, 0, pair, 1)
     for half in range(halves):
-        send_all(filt_out, filt_in, 0, half)
+        send_all(filt_out, filt_in, 1, half)
+
+    rim_copy.start()
+
+    def transform(landing, half):
+        def load(block):
+            def get():
+                value = landing[half, block]
+                angle = 2.0 * math.pi * block / (4 * devices)
+                return (value * math.cos(angle), value * math.sin(angle))
+
+            return get
+
+        for k, (real, imag) in enumerate(fft([load(b) for b in range(devices)], 1)):
+            cos, sin = (twist_cos[k : k + 1, :], twist_sin[k : k + 1, :])
+            rows = slice(k * SUB, (k + 1) * SUB)
+            spec_a[rows, :LANES] = real * cos - imag * sin
+            spec_a[rows, LANES:] = real * sin + imag * cos
+        return dot3(spec_a[...], fwd_hi, fwd_lo)
+
+    for pair in range(2):
+        wait_all(pair_in, recv_sems, 0, pair)
+    own_taps = tap_columns[me]
+
+    @pl.loop(0, devices // TOGETHER)
+    def _(step):
+        lane = lax.broadcasted_iota(jnp.int32, (TOGETHER, owned, LANES), 2)
+
+        def convolved(pair):
+            before = pair_in[pair, pl.ds(step * TOGETHER, TOGETHER)].astype(jnp.float32)
+            block = pair_in[pair, pl.ds(step * TOGETHER + 1, TOGETHER)].astype(jnp.float32)
+            total = None
+            for tap in range(taps):
+                moved = block
+                if tap:
+                    moved = pltpu.roll(jnp.where(lane >= LANES - tap, before, block), tap, 2)
+                column = pair * HALO + tap
+                term = own_taps[:, column : column + 1][None] * moved
+                total = term if total is None else total + term
+            return total
+
+        mixed = convolved(0) * convolved(1)
+        for half in range(halves):
+            rows = slice(half * SUB, (half + 1) * SUB)
+            mix_in[half, pl.ds(step * TOGETHER, TOGETHER)] = mixed[:, rows, :]
+
+    for half in range(halves):
+        spec_held[half] = transform(mix_in, half)
+
+    for half in range(halves):
+        wait_all(filt_in, recv_sems, 1, half)
+        far_spec = transform(filt_in, half)
+        far_re, far_im = (far_spec[:, :LANES], far_spec[:, LANES:])
+        held_re, held_im = (spec_held[half, :, :LANES], spec_held[half, :, LANES:])
+        spec_a[:, :LANES] = far_re * held_re - far_im * held_im
+        spec_a[:, LANES:] = far_re * held_im + far_im * held_re
+        spec_g[...] = dot3(spec_a[...], inv_hi, inv_lo)
+
+        def load(k):
+            def get():
+                rows = slice(k * SUB, (k + 1) * SUB)
+                real, imag = (spec_g[rows, :LANES], spec_g[rows, LANES:])
+                cos, sin = (twist_cos[k : k + 1, :], twist_sin[k : k + 1, :])
+                return (real * cos + imag * sin, imag * cos - real * sin)
+
+            return get
+
+        for block, (real, imag) in enumerate(fft([load(k) for k in range(devices)], -1)):
+            angle = 2.0 * math.pi * block / (4 * devices)
+            conv_out[half, block] = real * math.cos(angle) + imag * math.sin(angle)
+        send_all(conv_out, conv_in, 2, half)
 
     rim_copy.wait()
     keep = jnp.where(me > 0, 1.0, 0.0).astype(jnp.float32)
@@ -343,59 +435,9 @@
         return total
 
     for chunk in range(chunks):
-        mixed = shortened(1, chunk) * shortened(2, chunk)
-        direct[chunk] = mixed
-        scatter_rows(chunk, mixed.T, mix_out)
-    for half in range(halves):
-        send_all(mix_out, mix_in, 1, half)
-
-    for chunk in range(chunks):
         lanes = slice(chunk * LANES, (chunk + 1) * LANES)
         query[chunk] = shortened(0, chunk)
-        direct[chunk] = direct[chunk] * gain_ref[:, lanes]
-
-    def transform(landing, half):
-        def load(block):
-            def get():
-                value = landing[half, block]
-                angle = 2.0 * math.pi * block / (4 * devices)
-                return (value * math.cos(angle), value * math.sin(angle))
-
-            return get
-
-        for k, (real, imag) in enumerate(fft([load(b) for b in range(devices)], 1)):
-            cos, sin = (twist_cos[k : k + 1, :], twist_sin[k : k + 1, :])
-            rows = slice(k * SUB, (k + 1) * SUB)
-            spec_a[rows, :LANES] = real * cos - imag * sin
-            spec_a[rows, LANES:] = real * sin + imag * cos
-        return dot3(spec_a[...], fwd_hi, fwd_lo)
-
-    for half in range(halves):
-        wait_all(filt_in, recv_sems, 0, half)
-        spec_h[half] = transform(filt_in, half)
-
-    for half in range(halves):
-        wait_all(mix_in, recv_sems, 1, half)
-        mixed_spec = transform(mix_in, half)
-        mixed_re, mixed_im = (mixed_spec[:, :LANES], mixed_spec[:, LANES:])
-        filt_re, filt_im = (spec_h[half, :, :LANES], spec_h[half, :, LANES:])
-        spec_a[:, :LANES] = mixed_re * filt_re - mixed_im * filt_im
-        spec_a[:, LANES:] = mixed_re * filt_im + mixed_im * filt_re
-        spec_g[...] = dot3(spec_a[...], inv_hi, inv_lo)
-
-        def load(k):
-            def get():
-                rows = slice(k * SUB, (k + 1) * SUB)
-                real, imag = (spec_g[rows, :LANES], spec_g[rows, LANES:])
-                cos, sin = (twist_cos[k : k + 1, :], twist_sin[k : k + 1, :])
-                return (real * cos + imag * sin, imag * cos - real * sin)
-
-            return get
-
-        for block, (real, imag) in enumerate(fft([load(k) for k in range(devices)], -1)):
-            angle = 2.0 * math.pi * block / (4 * devices)
-            conv_out[half, block] = real * math.cos(angle) + imag * math.sin(angle)
-        send_all(conv_out, conv_in, 2, half)
+        direct[chunk] = shortened(1, chunk) * shortened(2, chunk) * gain_ref[:, lanes]
 
     for half in range(halves):
         wait_all(conv_in, recv_sems, 2, half)
@@ -408,9 +450,10 @@
         ]
         conv = jnp.concatenate(pieces, axis=0).T
         out_ref[:, lanes] = (query[chunk] * (conv + direct[chunk])).astype(out_ref.dtype)
+    for pair in range(2):
+        wait_all(pair_in, send_sems, 0, pair)
     for half in range(halves):
-        wait_all(filt_out, send_sems, 0, half)
-        wait_all(mix_out, send_sems, 1, half)
+        wait_all(filt_out, send_sems, 1, half)
         wait_all(conv_out, send_sems, 2, half)
 
 
@@ -457,17 +500,20 @@
             pltpu.VMEM((chunks, positions, LANES), f32),
             pltpu.VMEM((chunks, positions, LANES), f32),
             slabs,
+            pltpu.VMEM((2, devices, owned, LANES), bf16),
             slabs,
+            pltpu.VMEM((2, devices + 1, owned, LANES), bf16),
             slabs,
-            slabs,
+            pltpu.VMEM((LANES, LANES), f32),
+            pltpu.VMEM((devices, owned, LANES), f32),
             slabs,
             slabs,
             pltpu.VMEM((devices * SUB, 2 * LANES), f32),
             pltpu.VMEM((halves, devices * SUB, 2 * LANES), f32),
             pltpu.VMEM((devices * SUB, 2 * LANES), f32),
             pltpu.SemaphoreType.DMA((2,)),
-            pltpu.SemaphoreType.DMA((3, halves)),
-            pltpu.SemaphoreType.DMA((3, halves)),
+            pltpu.SemaphoreType.DMA((3, max(halves, 2))),
+            pltpu.SemaphoreType.DMA((3, max(halves, 2))),
         ],
         compiler_params=pltpu.CompilerParams(collective_id=0, has_side_effects=True),
     )(projections, short_taps, long_filter, skip_gain.reshape(1, channels), *consts)
@@ -482,7 +528,9 @@
         and channels % (SUB * devices) == 0
         and LANES % (channels // devices) == 0
         and devices & (devices - 1) == 0
-        and short_taps.shape[1] - 1 <= HALO
+        and (channels // devices) % 16 == 0
+        and devices % TOGETHER == 0
+        and short_taps.shape[1] <= HALO
     )
     if not fits:
         return per_device(projections, short_taps, long_filter, skip_gain)

time: 31.7 us -> 31.8 us (level)
  no operation moved by 1% of the time
where the time goes in v2:
time: 31.8 us; the launch traced here: 31.6 us
  Pallas kernels  30 us (94%)
  local copies, waits for them, and re-layouts  1.57 us (5%)
    pallas_call x1, Pallas kernels, owned_channels(): pl.pallas_call(functools.partial(owner_kernel, sizes), out_shape=jax.Shap...  30 us
    unnamed x1, local copies, waits for them, and re-layouts  1.57 us

profile of v2, /device:TPU:0, one launch (start us, length us, event | category | flops | bytes accessed | tf_op | source)
XLA Modules:
  0.0 31.6 jit_solution(17871544989264295322)
XLA Ops:
  0.0 30.0 %shard_map.100 = bf16[128,512]{1,0:T(8,128)(2,1)} custom-call(bf16[3,128,512]{2,1,0:T(8,128)(2,1)} %proj_ref.1, f32[3,7,512]{2,1,0:T(8,128)} %taps_ref.1, f32[128,512]{1,0:T(8,128)} %held_ref.1, f32[1,512]{1,0:T(1,128)} %bitcast.1, bf16[256,256]{1,0:T(8,128)(2,1)} %constant.12.clone.fwd_hi, bf16[256,256]{1,0:T(8,128)(2,1)} %constant.13.clone.fwd_lo, ...), custom_call_target="tpu_custom_call" | custom-call | tf_op jit(solution)/shard_map/pallas_call | solution.py:492
  30.0 1.6 %copy.12 = bf16[128,512]{1,0:T(8,128)(2,1)} copy(bf16[128,512]{1,0:T(8,128)(2,1)} %shard_map.100) | data formatting | bytes 262144

commit v3 on v2

--- a/solution.py
+++ b/solution.py
@@ -233,9 +233,20 @@
 
 def owner_kernel(
     sizes,
+    proj_ref_far,
+    taps_ref_far,
+    filt_ref_far,
+    gain_ref_far,
+    fwd_hi_far,
+    fwd_lo_far,
+    inv_hi_far,
+    inv_lo_far,
+    twist_cos_far,
+    twist_sin_far,
+    out_ref,
     proj_ref,
     taps_ref,
-    held_ref,
+    filt_ref,
     gain_ref,
     fwd_hi,
     fwd_lo,
@@ -243,7 +254,6 @@
     inv_lo,
     twist_cos,
     twist_sin,
-    out_ref,
     rim,
     ext,
     query,
@@ -260,6 +270,7 @@
     spec_a,
     spec_held,
     spec_g,
+    load_sems,
     rim_sems,
     send_sems,
     recv_sems,
@@ -295,9 +306,22 @@
                 first = part * owned + half * SUB
                 store[half, chunk * per_chunk + part] = turned_block[first : first + SUB, :]
 
+    far = (proj_ref_far, filt_ref_far, taps_ref_far, gain_ref_far, fwd_hi_far, fwd_lo_far)
+    far += (inv_hi_far, inv_lo_far, twist_cos_far, twist_sin_far)
+    near = (proj_ref, filt_ref, taps_ref, gain_ref, fwd_hi, fwd_lo)
+    near += (inv_hi, inv_lo, twist_cos, twist_sin)
+    loads = [
+        pltpu.make_async_copy(source_ref, here_ref, load_sems.at[which])
+        for which, (source_ref, here_ref) in enumerate(zip(far, near))
+    ]
+    for load in loads:
+        load.start()
+    for load in loads[:3]:
+        load.wait()
+
     for chunk in range(chunks):
         lanes = slice(chunk * LANES, (chunk + 1) * LANES)
-        scatter_rows(chunk, held_ref[:, lanes].T, filt_out)
+        scatter_rows(chunk, filt_ref[:, lanes].T, filt_out)
         for which in range(3):
             ext[which, chunk, HALO:, :] = proj_ref[which, :, lanes].astype(jnp.float32)
         tap_rows[...] = jnp.zeros_like(tap_rows)
@@ -313,6 +337,8 @@
     for pair in range(2):
         pair_in[pair, 0] = jnp.zeros((owned, LANES), jnp.bfloat16)
 
+    for load in loads[3:]:
+        load.wait()
     pl.semaphore_wait(barrier, devices - 1)
 
     rim_copy = pltpu.make_async_remote_copy(
@@ -487,14 +513,16 @@
     chunks = channels // LANES
     sizes = (groups, shards, positions, channels, short_taps.shape[1])
     f32, bf16 = (jnp.float32, jnp.bfloat16)
+    operands = (projections, short_taps, long_filter, skip_gain.reshape(1, channels), *consts)
     slabs = pltpu.VMEM((halves, devices, SUB, LANES), f32)
     vmem = pl.BlockSpec(memory_space=pltpu.VMEM)
     return pl.pallas_call(
         functools.partial(owner_kernel, sizes),
         out_shape=jax.ShapeDtypeStruct((positions, channels), bf16),
-        in_specs=[vmem] * (4 + len(consts)),
+        in_specs=[pl.BlockSpec(memory_space=pl.ANY)] * (4 + len(consts)),
         out_specs=vmem,
         scratch_shapes=[
+            *(pltpu.VMEM(operand.shape, operand.dtype) for operand in operands),
             pltpu.VMEM((3, HALO, channels), bf16),
             pltpu.VMEM((3, chunks, HALO + positions, LANES), f32),
             pltpu.VMEM((chunks, positions, LANES), f32),
@@ -511,12 +539,13 @@
             pltpu.VMEM((devices * SUB, 2 * LANES), f32),
             pltpu.VMEM((halves, devices * SUB, 2 * LANES), f32),
             pltpu.VMEM((devices * SUB, 2 * LANES), f32),
+            pltpu.SemaphoreType.DMA((len(operands),)),
             pltpu.SemaphoreType.DMA((2,)),
             pltpu.SemaphoreType.DMA((3, max(halves, 2))),
             pltpu.SemaphoreType.DMA((3, max(halves, 2))),
         ],
         compiler_params=pltpu.CompilerParams(collective_id=0, has_side_effects=True),
-    )(projections, short_taps, long_filter, skip_gain.reshape(1, channels), *consts)
+    )(*operands)
 
 
 def on_device(groups, shards, projections, short_taps, long_filter, skip_gain):

time: 31.8 us -> 30.5 us (0.959)
  Pallas kernels: 30 us -> 28.8 us
    pallas_call x1, Pallas kernels: 30 us -> 28.8 us  [owned_channels(): pl.pallas_call(functools.partial(owner_kernel, sizes), out_shape=jax.Shap...]
where the time goes in v3:
time: 30.5 us; the launch traced here: 30.4 us
  Pallas kernels  28.8 us (94%)
  local copies, waits for them, and re-layouts  1.57 us (5%)
    pallas_call x1, Pallas kernels, owned_channels(): pl.pallas_call(functools.partial(owner_kernel, sizes), out_shape=jax.Shap...  28.8 us
    unnamed x1, local copies, waits for them, and re-layouts  1.57 us

profile of v3, /device:TPU:0, one launch (start us, length us, event | category | flops | bytes accessed | tf_op | source)
XLA Modules:
  0.0 30.4 jit_solution(10410457995182273666)
XLA Ops:
  0.0 28.8 %shard_map.100 = bf16[128,512]{1,0:T(8,128)(2,1)} custom-call(bf16[3,128,512]{2,1,0:T(8,128)(2,1)} %proj_ref_far.1, f32[3,7,512]{2,1,0:T(8,128)} %taps_ref_far.1, f32[128,512]{1,0:T(8,128)} %filt_ref_far.1, f32[1,512]{1,0:T(1,128)} %bitcast.1, bf16[256,256]{1,0:T(8,128)(2,1)} %constant.12.clone.fwd_hi_far, bf16[256,256]{1,0:T(8,128)(2,1)} %constant.13.clone.fwd_lo_far, ...), custom_call_target="tpu_custom_call" | custom-call | tf_op jit(solution)/shard_map/pallas_call | solution.py:519
  28.8 1.6 %copy.12 = bf16[128,512]{1,0:T(8,128)(2,1)} copy(bf16[128,512]{1,0:T(8,128)(2,1)} %shard_map.100) | data formatting | bytes 262144
